TPU v7x, 512 devices: a whole 4x8x8 slice. The times are simulated.
512 devices in a mesh: dp: 16 (over z_hi, x, core), tensor: 32 (over z_lo, y).
Axes of the slice: x: 4, y: 8, z: 8 (z_hi: 2, z_lo: 4; z = z_hi * 4 + z_lo), core: 2. Of those that a mesh axis runs over, the one named last changes fastest.
Arguments:
- tokens: bfloat16 [8192, 4096], P(('dp', 'tensor')), parts along dimension 0, may hold values from -6 to 6
- norm_gain: float32 [4096], replicated, may hold values from 0.1 to 1.9
- gate_weight: bfloat16 [4096, 16384], P(None, 'tensor'), may hold values from -0.09375 to 0.09375
- up_weight: bfloat16 [4096, 16384], P(None, 'tensor'), may hold values from -0.09375 to 0.09375
- down_weight: bfloat16 [16384, 4096], P('tensor'), may hold values from -0.046875 to 0.046875
Outputs:
- mixed: bfloat16 [8192, 4096], P(('dp', 'tensor')), parts along dimension 0
There are 16 independent parts, one for each index of `dp`. A program takes and returns all parts, laid end to end along the dimension named above; an argument that names none is the same for every part. Nothing has to cross between parts.
All inputs are finite; a program needn't handle non-finite values.
Results may differ from a plain program's by a relative error of at most 0.023.
Values may be sent and summed in bfloat16 or wider, within the bound.
A program may use at most 64 MiB of HBM per device.

v0:
```python
import jax
import jax.numpy as jnp
from jax import lax
from jax.sharding import PartitionSpec as P


def on_device(tokens, norm_gain, gate_weight, up_weight, down_weight):
    values = tokens.astype(jnp.float32)
    scale = lax.rsqrt(jnp.mean(values * values, axis=1, keepdims=True) + 1e-05)
    normed = (values * scale * norm_gain[None, :]).astype(jnp.bfloat16)
    gathered = lax.all_gather(normed, "tensor", axis=0, tiled=True)
    gate = jnp.dot(gathered, gate_weight, preferred_element_type=jnp.float32)
    up = jnp.dot(gathered, up_weight, preferred_element_type=jnp.float32)
    hidden = (jax.nn.silu(gate) * up).astype(jnp.bfloat16)
    terms = jnp.dot(hidden, down_weight, preferred_element_type=jnp.float32)
    mixed = lax.psum_scatter(terms.astype(jnp.bfloat16), "tensor", scatter_dimension=0, tiled=True)
    return mixed


def solution(mesh):
    return jax.shard_map(
        on_device,
        mesh=mesh,
        in_specs=(
            P(("dp", "tensor"), None),
            P(),
            P(None, "tensor"),
            P(None, "tensor"),
            P("tensor", None),
        ),
        out_specs=P(("dp", "tensor"), None),
        check_vma=False,
    )
```

profile of v0, /device:TPU:2, one launch (start us, length us, event | category | flops | bytes accessed | tf_op | source)
XLA Modules:
  0.0 362.8 jit_solution(12300373263764878909)
XLA Ops:
  6.5 0.0 all-gather.2.cloned.1.call-start
  6.5 1.0 fusion.2
  7.6 1.7 fusion.4
  9.3 0.0 all-gather.2.cloned.1.call-update
  9.3 0.0 reduce-scatter.2.cloned.1.call-start
  9.3 163.4 %all-gather.2.cloned.1.call-done = bf16[512,4096]{1,0:T(8,128)(2,1)} async-done(((bf16[16,4096]{1,0:T(8,128)(2,1)}), bf16[512,4096]{1,0:T(8,128)(2,1)}) %all-gather.2.cloned.1.call-update) | async-done | bytes 4194320 | tf_op jit(solution)/shard_map/all_gather | solution.py:11
  172.8 5.8 %fusion.6 = f32[512,512]{1,0:T(8,128)S(1)} fusion(bf16[512,4096]{1,0:T(8,128)(2,1)} %all-gather.2.cloned.1.call-done, bf16[4096,512]{1,0:T(8,128)(2,1)} %param.7), kind=kOutput, calls=%fused_computation.11 | convolution fusion | flops 2147483648 | bytes 9437184 | tf_op jit(solution)/shard_map/dot_general | solution.py:12
  178.6 11.2 %convolution_convert_fusion = bf16[512,4096]{1,0:T(8,128)(2,1)} fusion(bf16[512,4096]{1,0:T(8,128)(2,1)} %param.9, bf16[512,4096]{1,0:T(8,128)(2,1)} %all-gather.2.cloned.1.call-done, bf16[4096,512]{1,0:T(8,128)(2,1)} %param.8, f32[512,512]{1,0:T(8,128)S(1)} %fusion.6), kind=kOutput, calls=%fused_computation | convolution fusion | flops 4298637312 | bytes 17825792 | tf_op jit(solution)/shard_map/dot_general | solution.py:15
  189.8 0.0 reduce-scatter.2.cloned.1.call-update
  189.8 166.1 %reduce-scatter.2.cloned.1.call-done = bf16[16,4096]{1,0:T(8,128)(2,1)} async-done(((bf16[512,4096]{1,0:T(8,128)(2,1)}), bf16[16,4096]{1,0:T(8,128)(2,1)}) %reduce-scatter.2.cloned.1.call-update) | async-done | bytes 131088 | tf_op jit(solution)/shard_map/reduce_scatter | solution.py:16
  (1 shorter events, 0.0 us)
Async XLA Ops:
  6.5 166.3 %all-gather.2.cloned.1.call-start = ((), (), s32[]{:S(2)}) async-start(), calls=%async_computation.1 | async-start | bytes 4325376 | tf_op jit(solution)/shard_map/all_gather | solution.py:11
  9.3 346.7 %reduce-scatter.2.cloned.1.call-start = ((), (), s32[]{:S(2)}) async-start(), calls=%async_computation.2 | async-start | bytes 4325376 | tf_op jit(solution)/shard_map/reduce_scatter | solution.py:16
Sparse Core Ops, SparseCore 0:
  9.4 163.3 all-gather.1
  190.0 165.9 reduce-scatter.1
where the time goes:
time: 363 us
  waiting for transfers between devices  330 us (91%)
  matrix products  17 us (5%)
  between operations  13.4 us (4%)
    reduce_scatter x1, waiting for transfers between devices, on_device(): lax.psum_scatter(terms.astype(jnp.bfloat16), 'tensor', scatter_dimension=...  166 us
    all_gather x1, waiting for transfers between devices, on_device(): gathered = lax.all_gather(normed, 'tensor', axis=0, tiled=True)  163 us
    dot_general x1, matrix products, on_device(): terms = jnp.dot(hidden, down_weight, preferred_element_type=jnp.float32)  11.2 us
  transfers between devices with their start and end apart: 2, of which 2 were waited for; matrix products, arithmetic and copies ran while one was open for 0% of the time, Pallas kernels for 0%

commit v1 on v0

v1 whole, which is shorter than its diff:
```python
import jax
import jax.numpy as jnp
from jax import lax
from jax.experimental import pallas as pl
from jax.experimental.pallas import tpu as pltpu
from jax.sharding import PartitionSpec as P

NZ, NY = 4, 8
F32, BF16 = jnp.float32, jnp.bfloat16
HOPS = NY // 2
GA, GB, RA, RB = range(4)
CHAINS = [(half, way) for half in (0, 1) for way in (0, 1)]


def kernel(
    tokens, gain, gate_hbm, up_hbm, down_hbm, out,
    xa, xb, pa, pb, hidden, gate_w, up_w, down_w,
    ring_a, ring_b, line_a, line_b,
    load_sem, ring_send, ring_recv, line_send, line_recv,
):
    me = lax.axis_index("tensor")
    z, y = me // NY, me % NY
    ca, cb = xa.shape[-1], xb.shape[-1]
    rows = tokens.shape[0]
    width = hidden.shape[-1]

    loads = [
        pltpu.make_async_copy(src, dst, load_sem.at[i])
        for i, (src, dst) in enumerate(((gate_hbm, gate_w), (up_hbm, up_w), (down_hbm, down_w)))
    ]
    for load in loads:
        load.start()

    def ring_next(way):
        return z * NY + (y + (1 if way else NY - 1)) % NY

    barrier = pltpu.get_barrier_semaphore()
    for way in (0, 1):
        pl.semaphore_signal(barrier, inc=1, device_id={"tensor": ring_next(way)})

    @pl.when(z > 0)
    def _():
        pl.semaphore_signal(barrier, inc=1, device_id={"tensor": me - NY})

    @pl.when(z < NZ - 1)
    def _():
        pl.semaphore_signal(barrier, inc=1, device_id={"tensor": me + NY})

    values = tokens[...].astype(F32)
    scale = lax.rsqrt(jnp.mean(values * values, axis=1, keepdims=True) + 1e-05)
    normed = (values * scale * gain[...]).astype(BF16)
    xa[z, y] = normed[:, :ca]
    xb[z, y] = normed[:, ca:]

    inside = (z > 0).astype(jnp.int32) + (z < NZ - 1).astype(jnp.int32)
    pl.semaphore_wait(barrier, 2 + inside)

    def cols(ref, half):
        c = ref.shape[-1] // 2
        return pl.ds(half * c, c)

    def region_ra(ref):
        return lambda yi, half: ref.at[:, yi, :, cols(ref, half)]

    def region_rb(ref):
        return lambda yi, half: ref.at[z, yi, :, cols(ref, half)]

    def region_la(ref):
        return lambda zi: ref.at[zi, y]

    def region_lb(ref):
        return lambda zi: ref.at[zi]

    def length(half, way):
        return HOPS if half == way else HOPS - 1

    def ring_copy(use, half, way, s, src, dst):
        return pltpu.make_async_remote_copy(
            src_ref=src, dst_ref=dst,
            send_sem=ring_send.at[use, half, way, s],
            recv_sem=ring_recv.at[use, half, way, s],
            device_id={"tensor": ring_next(way)},
        )

    def line_copy(use, way, s, src, dst):
        return pltpu.make_async_remote_copy(
            src_ref=src, dst_ref=dst,
            send_sem=line_send.at[use, way, s],
            recv_sem=line_recv.at[use, way, s],
            device_id={"tensor": me + (NY if way else -NY)},
        )

    def gather_ring(use, region):
        def block(way, s):
            return (y + (NY - s if way else s)) % NY

        def start(s):
            for half, way in CHAINS:
                if s < length(half, way):
                    ref = region(block(way, s), half)
                    ring_copy(use, half, way, s, ref, ref).start()

        def recv(s):
            for half, way in CHAINS:
                if s < length(half, way):
                    ref = region(block(way, s + 1), half)
                    ring_copy(use, half, way, s, ref, ref).wait_recv()

        def done():
            for half, way in CHAINS:
                for s in range(length(half, way)):
                    ref = region(block(way, s), half)
                    ring_copy(use, half, way, s, ref, ref).wait_send()

        return start, recv, done

    def rank(way):
        return z if way else NZ - 1 - z

    def place(way, q):
        return q if way else NZ - 1 - q

    def gather_line(use, region):
        def sends(way, s, act):
            q = rank(way)

            @pl.when((q >= s) & (q < NZ - 1))
            def _():
                ref = region(place(way, q - s))
                act(line_copy(use, way, s, ref, ref))

        def start(s):
            for way in (0, 1):
                sends(way, s, lambda c: c.start())

        def recv(s):
            for way in (0, 1):
                q = rank(way)

                @pl.when(q >= s + 1)
                def _():
                    ref = region(place(way, q - 1 - s))
                    line_copy(use, way, s, ref, ref).wait_recv()

        def done():
            for way in (0, 1):
                for s in range(NZ - 1):
                    sends(way, s, lambda c: c.wait_send())

        return start, recv, done

    def add(dst, src):
        dst[...] = (dst[...].astype(F32) + src[...].astype(F32)).astype(BF16)

    def scatter_ring(use, region, slots):
        def block(way, s):
            return (y + (HOPS - s if way else NY - HOPS + s)) % NY

        def first(half, way):
            return HOPS - length(half, way)

        def step(s):
            for half, way in CHAINS:
                f = first(half, way)
                if s < f:
                    continue
                ref = region(block(way, s), half)
                if s > f:
                    slot = slots.at[half, way, s - 1]
                    ring_copy(use, half, way, s - 1, slot, slot).wait_recv()
                    add(ref, slot)
                ring_copy(use, half, way, s, ref, slots.at[half, way, s]).start()

        def finish():
            for half, way in CHAINS:
                slot = slots.at[half, way, HOPS - 1]
                ring_copy(use, half, way, HOPS - 1, slot, slot).wait_recv()
                add(region(y, half), slot)

        def done():
            for half, way in CHAINS:
                for s in range(first(half, way), HOPS):
                    ref = region(block(way, s), half)
                    ring_copy(use, half, way, s, ref, slots.at[half, way, s]).wait_send()

        return step, finish, done

    def scatter_line(use, region, slots):
        last = NZ - 2

        def step(s):
            for way in (0, 1):
                q = rank(way)
                ref = region(place(way, NZ - 1 + q - s))
                if s > 0:

                    @pl.when((q >= 1) & (q <= s))
                    def _():
                        slot = slots.at[way, s - 1]
                        line_copy(use, way, s - 1, slot, slot).wait_recv()
                        add(ref, slot)

                @pl.when(q <= s)
                def _():
                    line_copy(use, way, s, ref, slots.at[way, s]).start()

        def finish():
            for way in (0, 1):

                @pl.when(rank(way) >= 1)
                def _():
                    slot = slots.at[way, last]
                    line_copy(use, way, last, slot, slot).wait_recv()
                    add(region(z), slot)

        def done():
            for way in (0, 1):
                for s in range(NZ - 1):
                    q = rank(way)

                    @pl.when(q <= s)
                    def _():
                        ref = region(place(way, NZ - 1 + q - s))
                        line_copy(use, way, s, ref, slots.at[way, s]).wait_send()

        return step, finish, done

    gla, gra = gather_line(GA, region_la(xa)), gather_ring(GA, region_ra(xa))
    grb, glb = gather_ring(GB, region_rb(xb)), gather_line(GB, region_lb(xb))
    gla[0](0)
    grb[0](0)
    for s in range(NZ - 1):
        gla[1](s)
        if s < NZ - 2:
            gla[0](s + 1)
        else:
            gra[0](0)
        grb[1](s)
        grb[0](s + 1)
    grb[1](HOPS - 1)
    glb[0](0)
    for s in range(HOPS):
        gra[1](s)
        if s < HOPS - 1:
            gra[0](s + 1)
        if s < NZ - 1:
            glb[1](s)
            if s < NZ - 2:
                glb[0](s + 1)
    for load in loads:
        load.wait()

    tile = min(256, width)
    deep = 2 * NY * rows

    def up_project(i, carry):
        m, n = i % 2, i // 2
        at = pl.ds(pl.multiple_of(n * tile, tile), tile)
        part = pl.ds(2 * m, 2)
        left, right = xa[part].reshape(deep, ca), xb[part].reshape(deep, cb)

        def dot(w):
            return jnp.dot(left, w[:ca, at], preferred_element_type=F32) + jnp.dot(
                right, w[ca:, at], preferred_element_type=F32
            )

        gate = dot(gate_w)
        h = gate / (1.0 + jnp.exp(-gate)) * dot(up_w)
        hidden[part, :, :, at] = h.astype(BF16).reshape(2, NY, rows, tile)
        return carry

    lax.fori_loop(0, 2 * (width // tile), up_project, 0)

    tile_a, tile_b = ca // 2, cb // 2

    def down_a(yi):
        h = hidden[:, yi].reshape(NZ * rows, width)

        def body(n, carry):
            at = pl.ds(pl.multiple_of(n * tile_a, 128), tile_a)
            part = jnp.dot(h, down_w[:, at], preferred_element_type=F32)
            pa[:, yi, :, at] = part.astype(BF16).reshape(NZ, rows, tile_a)
            return carry

        lax.fori_loop(0, 2, body, 0)

    def down_b(i, carry):
        zi, n = i // 2, i % 2
        h = hidden[zi].reshape(NY * rows, width)
        w_at = pl.ds(pl.multiple_of(ca + n * tile_b, 128), tile_b)
        at = pl.ds(pl.multiple_of(n * tile_b, 128), tile_b)
        part = jnp.dot(h, down_w[:, w_at], preferred_element_type=F32)
        pb[zi, :, :, at] = part.astype(BF16).reshape(NY, rows, tile_b)
        return carry

    sra, sla = scatter_ring(RA, region_ra(pa), ring_a), scatter_line(RA, region_la(pa), line_a)
    slb, srb = scatter_line(RB, region_lb(pb), line_b), scatter_ring(RB, region_rb(pb), ring_b)
    down_a((y + HOPS) % NY)
    sra[0](0)
    lax.fori_loop(0, 2 * NZ, down_b, 0)
    slb[0](0)
    for s in range(1, HOPS):
        down_a((y + HOPS - s) % NY)
        down_a((y + HOPS + s) % NY)
        if s == 1:
            down_a(y)
        sra[0](s)
        if s < NZ - 1:
            slb[0](s)
    slb[1]()
    srb[0](0)
    sra[1]()
    sla[0](0)
    for s in range(1, HOPS):
        srb[0](s)
        if s < NZ - 1:
            sla[0](s)
    sla[1]()
    srb[1]()
    out[:, :ca] = pa[z, y]
    out[:, ca:] = pb[z, y]
    for part in (gla, gra, grb, glb, sra, sla, slb, srb):
        part[2]()


def on_device(tokens, norm_gain, gate_weight, up_weight, down_weight):
    rows, d = tokens.shape
    width = gate_weight.shape[1]
    ca = d // 8 * 5
    cb = d - ca
    vmem, anywhere = (pl.BlockSpec(memory_space=space) for space in (pltpu.VMEM, pl.ANY))
    dma = pltpu.SemaphoreType.DMA
    return pl.pallas_call(
        kernel,
        out_shape=jax.ShapeDtypeStruct((rows, d), BF16),
        in_specs=[vmem, vmem, anywhere, anywhere, anywhere],
        out_specs=vmem,
        scratch_shapes=[
            pltpu.VMEM((NZ, NY, rows, ca), BF16),
            pltpu.VMEM((NZ, NY, rows, cb), BF16),
            pltpu.VMEM((NZ, NY, rows, ca), BF16),
            pltpu.VMEM((NZ, NY, rows, cb), BF16),
            pltpu.VMEM((NZ, NY, rows, width), BF16),
            pltpu.VMEM((d, width), BF16),
            pltpu.VMEM((d, width), BF16),
            pltpu.VMEM((width, d), BF16),
            pltpu.VMEM((2, 2, HOPS, NZ, rows, ca // 2), BF16),
            pltpu.VMEM((2, 2, HOPS, rows, cb // 2), BF16),
            pltpu.VMEM((2, NZ - 1, rows, ca), BF16),
            pltpu.VMEM((2, NZ - 1, NY, rows, cb), BF16),
            dma((3,)),
            dma((4, 2, 2, HOPS)),
            dma((4, 2, 2, HOPS)),
            dma((4, 2, NZ - 1)),
            dma((4, 2, NZ - 1)),
        ],
        compiler_params=pltpu.CompilerParams(
            collective_id=0, has_side_effects=True, vmem_limit_bytes=60 * 1024 * 1024
        ),
    )(tokens, norm_gain.reshape(1, d), gate_weight, up_weight, down_weight)


def solution(mesh):
    return jax.shard_map(
        on_device,
        mesh=mesh,
        in_specs=(
            P(("dp", "tensor"), None),
            P(),
            P(None, "tensor"),
            P(None, "tensor"),
            P("tensor", None),
        ),
        out_specs=P(("dp", "tensor"), None),
        check_vma=False,
    )
```

time: 363 us -> 104 us (0.29)
  the two profiles are of different devices: /device:TPU:2 before, /device:TPU:10 now
where the time goes in v1:
time: 104 us
  Pallas kernels  102 us (98%)
  local copies, waits for them, and re-layouts  1.57 us (2%)
    pallas_call x1, Pallas kernels, on_device(): pl.pallas_call(kernel, out_shape=jax.ShapeDtypeStruct((rows, d), BF16), i...  102 us

profile of v1, /device:TPU:10, one launch (start us, length us, event | category | flops | bytes accessed | tf_op | source)
XLA Modules:
  0.0 103.5 jit_solution(13192452653412315548)
XLA Ops:
  0.0 102.0 %shard_map.55 = bf16[16,4096]{1,0:T(8,128)(2,1)} custom-call(bf16[16,4096]{1,0:T(8,128)(2,1)} %tokens.1, f32[1,4096]{1,0:T(1,128)} %bitcast.1, bf16[4096,512]{1,0:T(8,128)(2,1)} %gate_hbm.1, bf16[4096,512]{1,0:T(8,128)(2,1)} %up_hbm.1, bf16[512,4096]{1,0:T(8,128)(2,1)} %down_hbm.1), custom_call_target="tpu_custom_call" | custom-call | tf_op jit(solution)/shard_map/pallas_call | solution.py:333
  102.0 1.6 %copy.7 = bf16[16,4096]{1,0:T(8,128)(2,1)} copy(bf16[16,4096]{1,0:T(8,128)(2,1)} %shard_map.55) | data formatting | bytes 262144

commit v2 on v0

v2 whole, which is shorter than its diff:
```python
import functools

import jax
import jax.numpy as jnp
from jax import lax
from jax.experimental import pallas as pl
from jax.experimental.pallas import tpu as pltpu
from jax.sharding import PartitionSpec as P

NZ = 4
F32, BF16 = jnp.float32, jnp.bfloat16
GA, GB, RA, RB = range(4)
FAR, RELAY, NEAR = range(3)
CHAINS = [(half, way) for half in (0, 1) for way in (0, 1)]


def kernel(
    n_dp, ny,
    tokens, gain, gate_hbm, up_hbm, down_hbm, out,
    xa, xb, pa, pb, acc, hidden, gate_w, up_w, down_w,
    ring_a, ring_b, line_a, line_b,
    load_sem, ring_send, ring_recv, line_send, line_recv,
):
    me, dp = lax.axis_index("tensor"), lax.axis_index("dp")
    z, y = me // ny, me % ny
    hops = ny // 2
    upper = n_dp // 2
    z_all = dp // upper * NZ + z
    turn = 1 - 2 * (dp % 2)
    ca, cb = xa.shape[-1], xb.shape[-1]
    rows = tokens.shape[0]
    width = hidden.shape[-1]

    loads = [
        pltpu.make_async_copy(src, dst, load_sem.at[i])
        for i, (src, dst) in enumerate(((gate_hbm, gate_w), (up_hbm, up_w), (down_hbm, down_w)))
    ]
    for load in loads:
        load.start()

    def ring_next(way):
        return {"dp": dp, "tensor": z * ny + (y + (1 if way else ny - 1)) % ny}

    def line_next(ahead):
        to = (z_all + 2 * NZ + (turn if ahead else -turn)) % (2 * NZ)
        return {"dp": dp % upper + to // NZ * upper, "tensor": to % NZ * ny + y}

    barrier = pltpu.get_barrier_semaphore()
    for way in (0, 1):
        pl.semaphore_signal(barrier, inc=1, device_id=ring_next(way))
        pl.semaphore_signal(barrier, inc=1, device_id=line_next(way))

    values = tokens[...].astype(F32)
    scale = lax.rsqrt(jnp.mean(values * values, axis=1, keepdims=True) + 1e-05)
    normed = (values * scale * gain[...]).astype(BF16)
    xa[0, y] = normed[:, :ca]
    xb[0, y] = normed[:, ca:]

    pl.semaphore_wait(barrier, 4)

    def cols(ref, half):
        c = ref.shape[-1] // 2
        return pl.ds(half * c, c)

    def region_ra(ref):
        return lambda yi, half: ref.at[:, yi, :, cols(ref, half)]

    def region_rb(ref):
        return lambda yi, half: ref.at[0, yi, :, cols(ref, half)]

    def region_la(ref):
        return lambda slot, piece: ref.at[slot, y]

    def region_lb(ref):
        return lambda slot, piece: ref.at[slot, pl.ds(piece * hops, hops)]

    def length(half, way):
        return hops if half == way else hops - 1

    def ring_copy(use, half, way, s, src, dst):
        return pltpu.make_async_remote_copy(
            src_ref=src, dst_ref=dst,
            send_sem=ring_send.at[use, half, way, s],
            recv_sem=ring_recv.at[use, half, way, s],
            device_id=ring_next(way),
        )

    def line_copy(use, kind, piece, ahead, src, dst):
        return pltpu.make_async_remote_copy(
            src_ref=src, dst_ref=dst,
            send_sem=line_send.at[use, kind, piece],
            recv_sem=line_recv.at[use, kind, piece],
            device_id=line_next(ahead),
        )

    def gather_ring(use, region):
        def block(way, s):
            return (y + (ny - s if way else s)) % ny

        def start(s):
            for half, way in CHAINS:
                if s < length(half, way):
                    ref = region(block(way, s), half)
                    ring_copy(use, half, way, s, ref, ref).start()

        def recv(s):
            for half, way in CHAINS:
                if s < length(half, way):
                    ref = region(block(way, s + 1), half)
                    ring_copy(use, half, way, s, ref, ref).wait_recv()

        def done():
            for half, way in CHAINS:
                for s in range(length(half, way)):
                    ref = region(block(way, s), half)
                    ring_copy(use, half, way, s, ref, ref).wait_send()

        return start, recv, done

    def gather_line(use, region):
        def copy(kind, piece):
            src, dst = {FAR: (0, 1), RELAY: (1, 2), NEAR: (0, 3)}[kind]
            return line_copy(use, kind, piece, kind != NEAR, region(src, piece), region(dst, piece))

        return copy

    def scatter_line(use, region, slots):
        def copy(kind, piece):
            src = {FAR: 2, RELAY: 1, NEAR: 3}[kind]
            dst = region_of(slots, kind, piece)
            return line_copy(use, kind, piece, kind == NEAR, region(src, piece), dst)

        def region_of(ref, kind, piece):
            return ref.at[kind] if use == RA else ref.at[kind, pl.ds(piece * hops, hops)]

        def relay(piece):
            copy(FAR, piece).wait_recv()
            add(region(1, piece), region_of(slots, FAR, piece))
            copy(RELAY, piece).start()

        def finish(piece):
            for kind in (NEAR, RELAY):
                copy(kind, piece).wait_recv()
                add(region(0, piece), region_of(slots, kind, piece))

        return copy, relay, finish

    def add(dst, src):
        dst[...] = (dst[...].astype(F32) + src[...].astype(F32)).astype(BF16)

    def scatter_ring(use, region, slots):
        def block(way, s):
            return (y + (hops - s if way else ny - hops + s)) % ny

        def first(half, way):
            return hops - length(half, way)

        def step(s):
            for half, way in CHAINS:
                f = first(half, way)
                if s < f:
                    continue
                ref = region(block(way, s), half)
                if s > f:
                    slot = slots.at[half, way, s - 1]
                    ring_copy(use, half, way, s - 1, slot, slot).wait_recv()
                    add(ref, slot)
                ring_copy(use, half, way, s, ref, slots.at[half, way, s]).start()

        def finish():
            for half, way in CHAINS:
                slot = slots.at[half, way, hops - 1]
                ring_copy(use, half, way, hops - 1, slot, slot).wait_recv()
                add(region(y, half), slot)

        def done():
            for half, way in CHAINS:
                for s in range(first(half, way), hops):
                    ref = region(block(way, s), half)
                    ring_copy(use, half, way, s, ref, slots.at[half, way, s]).wait_send()

        return step, finish, done

    gla, gra = gather_line(GA, region_la(xa)), gather_ring(GA, region_ra(xa))
    grb, glb = gather_ring(GB, region_rb(xb)), gather_line(GB, region_lb(xb))
    gla(FAR, 0).start()
    gla(NEAR, 0).start()
    grb[0](0)
    acc[...] = jnp.zeros_like(acc)
    gla(FAR, 0).wait_recv()
    gla(RELAY, 0).start()
    grb[1](0)
    grb[0](1)
    gla(NEAR, 0).wait_recv()
    gla(RELAY, 0).wait_recv()
    gra[0](0)
    for s in range(1, hops):
        grb[1](s)
        if s < hops - 1:
            grb[0](s + 1)
    for piece in (0, 1):
        glb(FAR, piece).start()
    for piece in (0, 1):
        glb(NEAR, piece).start()

    tile = min(256, width)

    def up_project(load, lo, size, store):
        def body(n, carry):
            at = pl.ds(pl.multiple_of(n * tile, tile), tile)
            left = load()
            for i, w in enumerate((gate_w, up_w)):
                store(i, at, jnp.dot(left, w[lo : lo + size, at], preferred_element_type=F32))
            return carry

        lax.fori_loop(0, width // tile, body, 0)

    def up_a(*groups):
        def load():
            return jnp.concatenate([xa[:, yi].reshape(NZ * rows, ca) for yi in groups], axis=0)

        def store(i, at, part):
            parts = part.reshape(len(groups), NZ, rows, tile)
            for g, yi in enumerate(groups):
                acc[i, :, yi, :, at] += parts[g]

        up_project(load, 0, ca, store)

    def up_b(slot):
        def store(i, at, part):
            acc[i, slot, :, :, at] += part.reshape(ny, rows, tile)

        up_project(lambda: xb[slot].reshape(ny * rows, cb), ca, cb, store)

    loads[0].wait()
    loads[1].wait()
    up_a(y)
    for s in range(hops):
        gra[1](s)
        if s < hops - 1:
            gra[0](s + 1)
        if s >= hops - 3 and s < hops - 1:
            piece = s - (hops - 3)
            glb(FAR, piece).wait_recv()
            glb(RELAY, piece).start()
        if s < hops - 1:
            up_a((y + s + 1) % ny, (y + ny - s - 1) % ny)
        if s == 0:
            up_b(0)
        if s == hops - 2:
            up_b(1)
    for piece in (0, 1):
        glb(NEAR, piece).wait_recv()
    up_a((y + hops) % ny)
    up_b(3)
    for piece in (0, 1):
        glb(RELAY, piece).wait_recv()
    up_b(2)

    def activate(i, carry):
        gate, up = acc[0, i // ny, i % ny], acc[1, i // ny, i % ny]
        hidden[i // ny, i % ny] = (gate / (1.0 + jnp.exp(-gate)) * up).astype(BF16)
        return carry

    lax.fori_loop(0, NZ * ny, activate, 0, unroll=4)
    loads[2].wait()
    tile_a, tile_b = ca // 2, cb // 2

    def down_a(yi):
        h = hidden[:, yi].reshape(NZ * rows, width)

        def body(n, carry):
            at = pl.ds(pl.multiple_of(n * tile_a, 128), tile_a)
            part = jnp.dot(h, down_w[:, at], preferred_element_type=F32)
            pa[:, yi, :, at] = part.astype(BF16).reshape(NZ, rows, tile_a)
            return carry

        lax.fori_loop(0, 2, body, 0)

    def down_b(slot):
        h = hidden[slot].reshape(ny * rows, width)

        def body(n, carry):
            w_at = pl.ds(pl.multiple_of(ca + n * tile_b, 128), tile_b)
            at = pl.ds(pl.multiple_of(n * tile_b, 128), tile_b)
            part = jnp.dot(h, down_w[:, w_at], preferred_element_type=F32)
            pb[slot, :, :, at] = part.astype(BF16).reshape(ny, rows, tile_b)
            return carry

        lax.fori_loop(0, 2, body, 0)

    sra, sla = scatter_ring(RA, region_ra(pa), ring_a), scatter_line(RA, region_la(pa), line_a)
    slb, srb = scatter_line(RB, region_lb(pb), line_b), scatter_ring(RB, region_rb(pb), ring_b)
    down_a((y + hops) % ny)
    sra[0](0)
    for slot, kind in ((2, FAR), (3, NEAR)):
        down_b(slot)
        for piece in (0, 1):
            slb[0](kind, piece).start()
    down_b(1)
    for s in range(1, hops):
        down_a((y + hops - s) % ny)
        down_a((y + hops + s) % ny)
        if s == 1:
            down_b(0)
        if s == hops - 1:
            down_a(y)
        sra[0](s)
        if s >= hops - 3 and s < hops - 1:
            slb[1](s - (hops - 3))
    sra[1]()
    sla[0](FAR, 0).start()
    sla[0](NEAR, 0).start()
    for piece in (0, 1):
        slb[2](piece)
    srb[0](0)
    sla[1](0)
    for s in range(1, hops):
        srb[0](s)
    sla[2](0)
    srb[1]()
    out[:, :ca] = pa[0, y]
    out[:, ca:] = pb[0, y]
    for kind in (FAR, RELAY, NEAR):
        gla(kind, 0).wait_send()
        sla[0](kind, 0).wait_send()
        for piece in (0, 1):
            glb(kind, piece).wait_send()
            slb[0](kind, piece).wait_send()
    for part in (gra, grb, sra, srb):
        part[2]()


def on_device(n_dp, n_tensor, tokens, norm_gain, gate_weight, up_weight, down_weight):
    rows, d = tokens.shape
    width = gate_weight.shape[1]
    ny = n_tensor // NZ
    hops = ny // 2
    ca = d // 16 * 7
    cb = d - ca
    vmem, anywhere = (pl.BlockSpec(memory_space=space) for space in (pltpu.VMEM, pl.ANY))
    dma = pltpu.SemaphoreType.DMA
    return pl.pallas_call(
        functools.partial(kernel, n_dp, ny),
        out_shape=jax.ShapeDtypeStruct((rows, d), BF16),
        in_specs=[vmem, vmem, anywhere, anywhere, anywhere],
        out_specs=vmem,
        scratch_shapes=[
            pltpu.VMEM((NZ, ny, rows, ca), BF16),
            pltpu.VMEM((NZ, ny, rows, cb), BF16),
            pltpu.VMEM((NZ, ny, rows, ca), BF16),
            pltpu.VMEM((NZ, ny, rows, cb), BF16),
            pltpu.VMEM((2, NZ, ny, rows, width), F32),
            pltpu.VMEM((NZ, ny, rows, width), BF16),
            pltpu.VMEM((d, width), BF16),
            pltpu.VMEM((d, width), BF16),
            pltpu.VMEM((width, d), BF16),
            pltpu.VMEM((2, 2, hops, NZ, rows, ca // 2), BF16),
            pltpu.VMEM((2, 2, hops, rows, cb // 2), BF16),
            pltpu.VMEM((3, rows, ca), BF16),
            pltpu.VMEM((3, ny, rows, cb), BF16),
            dma((3,)),
            dma((4, 2, 2, hops)),
            dma((4, 2, 2, hops)),
            dma((4, 3, 2)),
            dma((4, 3, 2)),
        ],
        compiler_params=pltpu.CompilerParams(
            collective_id=0, has_side_effects=True, vmem_limit_bytes=60 * 1024 * 1024
        ),
    )(tokens, norm_gain.reshape(1, d), gate_weight, up_weight, down_weight)


def solution(mesh):
    return jax.shard_map(
        functools.partial(on_device, mesh.shape["dp"], mesh.shape["tensor"]),
        mesh=mesh,
        in_specs=(
            P(("dp", "tensor"), None),
            P(),
            P(None, "tensor"),
            P(None, "tensor"),
            P("tensor", None),
        ),
        out_specs=P(("dp", "tensor"), None),
        check_vma=False,
    )
```

time: 363 us -> 94.1 us (0.26)
  the two profiles are of different devices: /device:TPU:2 before, /device:TPU:4 now
where the time goes in v2:
time: 94.1 us; the launch traced here: 94 us
  Pallas kernels  92.4 us (98%)
  local copies, waits for them, and re-layouts  1.57 us (2%)
    pallas_call x1, Pallas kernels, on_device(): pl.pallas_call(functools.partial(kernel, n_dp, ny), out_shape=jax.ShapeDt...  92.4 us

profile of v2, /device:TPU:4, one launch (start us, length us, event | category | flops | bytes accessed | tf_op | source)
XLA Modules:
  0.0 94.0 jit_solution(17778673444758054274)
XLA Ops:
  0.0 92.4 %shard_map.55 = bf16[16,4096]{1,0:T(8,128)(2,1)} custom-call(bf16[16,4096]{1,0:T(8,128)(2,1)} %tokens.1, f32[1,4096]{1,0:T(1,128)} %bitcast.1, bf16[4096,512]{1,0:T(8,128)(2,1)} %gate_hbm.1, bf16[4096,512]{1,0:T(8,128)(2,1)} %up_hbm.1, bf16[512,4096]{1,0:T(8,128)(2,1)} %down_hbm.1), custom_call_target="tpu_custom_call" | custom-call | tf_op jit(solution)/shard_map/pallas_call | solution.py:343
  92.4 1.6 %copy.7 = bf16[16,4096]{1,0:T(8,128)(2,1)} copy(bf16[16,4096]{1,0:T(8,128)(2,1)} %shard_map.55) | data formatting | bytes 262144

commit v3 on v2

v3 whole, which is shorter than its diff:
```python
import functools

import jax
import jax.numpy as jnp
from jax import lax
from jax.experimental import pallas as pl
from jax.experimental.pallas import tpu as pltpu
from jax.sharding import PartitionSpec as P

NZ = 4
F32, BF16 = jnp.float32, jnp.bfloat16
GA, GB, RA, RB = 0, 4, 5, 9
LGA, LGB, LRA, LRB = range(4)
FAR, RELAY, NEAR = range(3)
CHAINS = [(half, way) for half in (0, 1) for way in (0, 1)]


def kernel(
    n_dp, ny,
    tokens, gain, gate_hbm, up_hbm, down_hbm, out,
    xa, xb, pa, pb, hidden, gate_w, up_w, down_w,
    ring_a, ring_b, line_a, line_b,
    load_sem, ring_send, ring_recv, line_send, line_recv,
):
    me, dp = lax.axis_index("tensor"), lax.axis_index("dp")
    z, y = me // ny, me % ny
    hops = ny // 2
    upper = n_dp // 2
    z_all = dp // upper * NZ + z
    turn = 1 - 2 * (dp % 2)
    ca, cb = xa.shape[-1], xb.shape[-1]
    rows = tokens.shape[0]
    width = hidden.shape[-1]

    loads = [
        pltpu.make_async_copy(src, dst, load_sem.at[i])
        for i, (src, dst) in enumerate(((gate_hbm, gate_w), (up_hbm, up_w), (down_hbm, down_w)))
    ]
    for load in loads:
        load.start()

    def ring_next(way):
        return {"dp": dp, "tensor": z * ny + (y + (1 if way else ny - 1)) % ny}

    def line_next(ahead):
        to = (z_all + 2 * NZ + (turn if ahead else -turn)) % (2 * NZ)
        return {"dp": dp % upper + to // NZ * upper, "tensor": to % NZ * ny + y}

    barrier = pltpu.get_barrier_semaphore()
    for way in (0, 1):
        pl.semaphore_signal(barrier, inc=1, device_id=ring_next(way))
        pl.semaphore_signal(barrier, inc=1, device_id=line_next(way))

    values = tokens[...].astype(F32)
    scale = lax.rsqrt(jnp.mean(values * values, axis=1, keepdims=True) + 1e-05)
    normed = (values * scale * gain[...]).astype(BF16)
    xa[0, y] = normed[:, :ca]
    xb[0, y] = normed[:, ca:]

    pl.semaphore_wait(barrier, 4)

    def cols(ref, half):
        c = ref.shape[-1] // 2
        return pl.ds(half * c, c)

    def on_ring(ref, slot):
        return lambda yi, half: ref.at[slot, yi, :, cols(ref, half)]

    def near_y(d):
        return [(y + e) % ny for e in sorted({d, (ny - d) % ny}, reverse=True)]

    def pieces(d):
        return [(2 * d - 1 + i if d else 0, yi) for i, yi in enumerate(near_y(d))]

    def length(half, way):
        return hops if half == way else hops - 1

    def ring_copy(use, half, way, s, src, dst):
        return pltpu.make_async_remote_copy(
            src_ref=src, dst_ref=dst,
            send_sem=ring_send.at[use, half, way, s],
            recv_sem=ring_recv.at[use, half, way, s],
            device_id=ring_next(way),
        )

    def line_copy(use, kind, piece, ahead, src, dst):
        return pltpu.make_async_remote_copy(
            src_ref=src, dst_ref=dst,
            send_sem=line_send.at[use, kind, piece],
            recv_sem=line_recv.at[use, kind, piece],
            device_id=line_next(ahead),
        )

    def gather_ring(use, region):
        def block(way, s):
            return (y + (ny - s if way else s)) % ny

        def start(s):
            for half, way in CHAINS:
                if s < length(half, way):
                    ref = region(block(way, s), half)
                    ring_copy(use, half, way, s, ref, ref).start()

        def recv(s):
            for half, way in CHAINS:
                if s < length(half, way):
                    ref = region(block(way, s + 1), half)
                    ring_copy(use, half, way, s, ref, ref).wait_recv()

        def done():
            for half, way in CHAINS:
                for s in range(length(half, way)):
                    ref = region(block(way, s), half)
                    ring_copy(use, half, way, s, ref, ref).wait_send()

        return start, recv, done

    def gather_line(use, ref):
        def copy(kind, piece, yi):
            src, dst = {FAR: (0, 1), RELAY: (1, 2), NEAR: (0, 3)}[kind]
            return line_copy(use, kind, piece, kind != NEAR, ref.at[src, yi], ref.at[dst, yi])

        return copy

    def scatter_line(use, ref, slots):
        def copy(kind, piece, yi):
            src = {FAR: 2, RELAY: 1, NEAR: 3}[kind]
            return line_copy(use, kind, piece, kind == NEAR, ref.at[src, yi], slots.at[kind, piece])

        def relay(piece, yi):
            copy(FAR, piece, yi).wait_recv()
            add(ref.at[1, yi], slots.at[FAR, piece])
            copy(RELAY, piece, yi).start()

        def finish(piece, yi):
            for kind in (NEAR, RELAY):
                copy(kind, piece, yi).wait_recv()
                add(ref.at[0, yi], slots.at[kind, piece])

        return copy, relay, finish

    def add(dst, src):
        dst[...] = (dst[...].astype(F32) + src[...].astype(F32)).astype(BF16)

    def scatter_ring(use, region, slots):
        def block(way, s):
            return (y + (hops - s if way else ny - hops + s)) % ny

        def first(half, way):
            return hops - length(half, way)

        def step(s):
            for half, way in CHAINS:
                f = first(half, way)
                if s < f:
                    continue
                ref = region(block(way, s), half)
                if s > f:
                    slot = slots.at[half, way, s - 1]
                    ring_copy(use, half, way, s - 1, slot, slot).wait_recv()
                    add(ref, slot)
                ring_copy(use, half, way, s, ref, slots.at[half, way, s]).start()

        def finish():
            for half, way in CHAINS:
                slot = slots.at[half, way, hops - 1]
                ring_copy(use, half, way, hops - 1, slot, slot).wait_recv()
                add(region(y, half), slot)

        def done():
            for half, way in CHAINS:
                for s in range(first(half, way), hops):
                    ref = region(block(way, s), half)
                    ring_copy(use, half, way, s, ref, slots.at[half, way, s]).wait_send()

        return step, finish, done

    tile = min(256, width)

    def up_project(d):
        groups = near_y(d)
        deep = len(groups) * NZ * rows

        def body(n, carry):
            at = pl.ds(pl.multiple_of(n * tile, tile), tile)
            left, right = (
                jnp.concatenate([x[:, yi].reshape(NZ * rows, x.shape[-1]) for yi in groups], axis=0)
                for x in (xa, xb)
            )

            def dot(w):
                return jnp.dot(left, w[:ca, at], preferred_element_type=F32) + jnp.dot(
                    right, w[ca:, at], preferred_element_type=F32
                )

            gate = dot(gate_w)
            h = (gate / (1.0 + jnp.exp(-gate)) * dot(up_w)).astype(BF16)
            h = h.reshape(len(groups), NZ, rows, tile)
            for g, yi in enumerate(groups):
                hidden[:, yi, :, at] = h[g]
            return carry

        lax.fori_loop(0, width // tile, body, 0)

    gla, glb = gather_line(LGA, xa), gather_line(LGB, xb)
    gra = [gather_ring(GA + slot, on_ring(xa, slot)) for slot in range(NZ)]
    grb = gather_ring(GB, on_ring(xb, 0))
    begins = (0, 1, 2, 1)

    def ring_tick(ring, t):
        if 0 < t <= hops:
            ring[1](t - 1)
        if 0 <= t < hops:
            ring[0](t)

    for t in range(hops + 3):
        if t == 0:
            gla(FAR, 0, y).start()
            gla(NEAR, 0, y).start()
        if t == 1:
            gla(FAR, 0, y).wait_recv()
            gla(RELAY, 0, y).start()
            gla(NEAR, 0, y).wait_recv()
        if t == 2:
            gla(RELAY, 0, y).wait_recv()
        ring_tick(grb, t)
        if t <= hops:
            for piece, yi in pieces(t):
                glb(FAR, piece, yi).start()
        if 1 <= t <= hops + 1:
            for piece, yi in pieces(t - 1):
                glb(FAR, piece, yi).wait_recv()
                glb(RELAY, piece, yi).start()
        if t <= hops:
            for piece, yi in pieces(t):
                glb(NEAR, piece, yi).start()
        for slot in (0, 1, 3, 2):
            ring_tick(gra[slot], t - begins[slot])
        if t == 2:
            loads[0].wait()
            loads[1].wait()
        if t >= 2:
            for piece, yi in pieces(t - 2):
                glb(NEAR, piece, yi).wait_recv()
                glb(RELAY, piece, yi).wait_recv()
            up_project(t - 2)

    loads[2].wait()
    down_tiles = [(pa, 0, ca), (pb, ca, cb)]

    def down(d):
        groups = near_y(d)
        h = jnp.concatenate([hidden[:, yi].reshape(NZ * rows, width) for yi in groups], axis=0)
        for dst, lo, size in down_tiles:
            half = size // 2

            def body(n, carry):
                w_at = pl.ds(pl.multiple_of(lo + n * half, 128), half)
                at = pl.ds(pl.multiple_of(n * half, 128), half)
                part = jnp.dot(h, down_w[:, w_at], preferred_element_type=F32)
                part = part.astype(BF16).reshape(len(groups), NZ, rows, half)
                for g, yi in enumerate(groups):
                    dst[:, yi, :, at] = part[g]
                return carry

            lax.fori_loop(0, 2, body, 0)

    sla, slb = scatter_line(LRA, pa, line_a), scatter_line(LRB, pb, line_b)
    sra = [scatter_ring(RA + slot, on_ring(pa, slot), ring_a.at[slot]) for slot in range(NZ)]
    srb = scatter_ring(RB, on_ring(pb, 0), ring_b)
    waits = (2, 1, 0, 1)

    def back_tick(ring, t):
        if 0 <= t < hops:
            ring[0](t)
        if t == hops:
            ring[1]()

    down(hops)
    for t in range(hops + 3):
        for slot in (2, 1, 3, 0):
            back_tick(sra[slot], t - waits[slot])
            if slot == 2 and t == hops:
                sla[0](FAR, 0, y).start()
            if slot == 1 and t == hops + 1:
                sla[1](0, y)
            if slot == 3 and t == hops + 1:
                sla[0](NEAR, 0, y).start()
        if t <= hops:
            for piece, yi in pieces(hops - t):
                slb[0](FAR, piece, yi).start()
        if 1 <= t <= hops + 1:
            for piece, yi in pieces(hops + 1 - t):
                slb[1](piece, yi)
        if t <= hops:
            for piece, yi in pieces(hops - t):
                slb[0](NEAR, piece, yi).start()
        if t < hops:
            down(hops - 1 - t)
        if t >= 2:
            for piece, yi in pieces(hops + 2 - t):
                slb[2](piece, yi)
            back_tick(srb, t - 2)
    sla[2](0, y)
    out[:, :ca] = pa[0, y]
    out[:, ca:] = pb[0, y]
    for kind in (FAR, RELAY, NEAR):
        gla(kind, 0, y).wait_send()
        sla[0](kind, 0, y).wait_send()
        for d in range(hops + 1):
            for piece, yi in pieces(d):
                glb(kind, piece, yi).wait_send()
                slb[0](kind, piece, yi).wait_send()
    for part in (*gra, grb, *sra, srb):
        part[2]()


def on_device(n_dp, n_tensor, tokens, norm_gain, gate_weight, up_weight, down_weight):
    rows, d = tokens.shape
    width = gate_weight.shape[1]
    ny = n_tensor // NZ
    hops = ny // 2
    ca = d // 16 * 7
    cb = d - ca
    vmem, anywhere = (pl.BlockSpec(memory_space=space) for space in (pltpu.VMEM, pl.ANY))
    dma = pltpu.SemaphoreType.DMA
    return pl.pallas_call(
        functools.partial(kernel, n_dp, ny),
        out_shape=jax.ShapeDtypeStruct((rows, d), BF16),
        in_specs=[vmem, vmem, anywhere, anywhere, anywhere],
        out_specs=vmem,
        scratch_shapes=[
            pltpu.VMEM((NZ, ny, rows, ca), BF16),
            pltpu.VMEM((NZ, ny, rows, cb), BF16),
            pltpu.VMEM((NZ, ny, rows, ca), BF16),
            pltpu.VMEM((NZ, ny, rows, cb), BF16),
            pltpu.VMEM((NZ, ny, rows, width), BF16),
            pltpu.VMEM((d, width), BF16),
            pltpu.VMEM((d, width), BF16),
            pltpu.VMEM((width, d), BF16),
            pltpu.VMEM((NZ, 2, 2, hops, rows, ca // 2), BF16),
            pltpu.VMEM((2, 2, hops, rows, cb // 2), BF16),
            pltpu.VMEM((3, 1, rows, ca), BF16),
            pltpu.VMEM((3, ny, rows, cb), BF16),
            dma((3,)),
            dma((10, 2, 2, hops)),
            dma((10, 2, 2, hops)),
            dma((4, 3, ny)),
            dma((4, 3, ny)),
        ],
        compiler_params=pltpu.CompilerParams(
            collective_id=0, has_side_effects=True, vmem_limit_bytes=60 * 1024 * 1024
        ),
    )(tokens, norm_gain.reshape(1, d), gate_weight, up_weight, down_weight)


def solution(mesh):
    return jax.shard_map(
        functools.partial(on_device, mesh.shape["dp"], mesh.shape["tensor"]),
        mesh=mesh,
        in_specs=(
            P(("dp", "tensor"), None),
            P(),
            P(None, "tensor"),
            P(None, "tensor"),
            P("tensor", None),
        ),
        out_specs=P(("dp", "tensor"), None),
        check_vma=False,
    )
```

time: 94.1 us -> 80.8 us (0.86)
  Pallas kernels: 92.4 us -> 79.1 us
    pallas_call x1, Pallas kernels: 92.4 us -> 79.1 us  [on_device(): pl.pallas_call(functools.partial(kernel, n_dp, ny), out_shape=jax.ShapeDt...]
where the time goes in v3:
time: 80.8 us; the launch traced here: 80.7 us
  Pallas kernels  79.1 us (98%)
  local copies, waits for them, and re-layouts  1.57 us (2%)
    pallas_call x1, Pallas kernels, on_device(): pl.pallas_call(functools.partial(kernel, n_dp, ny), out_shape=jax.ShapeDt...  79.1 us

profile of v3, /device:TPU:4, one launch (start us, length us, event | category | flops | bytes accessed | tf_op | source)
XLA Modules:
  0.0 80.7 jit_solution(3175648673306928554)
XLA Ops:
  0.0 79.1 %shard_map.55 = bf16[16,4096]{1,0:T(8,128)(2,1)} custom-call(bf16[16,4096]{1,0:T(8,128)(2,1)} %tokens.1, f32[1,4096]{1,0:T(1,128)} %bitcast.1, bf16[4096,512]{1,0:T(8,128)(2,1)} %gate_hbm.1, bf16[4096,512]{1,0:T(8,128)(2,1)} %up_hbm.1, bf16[512,4096]{1,0:T(8,128)(2,1)} %down_hbm.1), custom_call_target="tpu_custom_call" | custom-call | tf_op jit(solution)/shard_map/pallas_call | solution.py:327
  79.1 1.6 %copy.7 = bf16[16,4096]{1,0:T(8,128)(2,1)} copy(bf16[16,4096]{1,0:T(8,128)(2,1)} %shard_map.55) | data formatting | bytes 262144
